TPU v7x, 512 devices: a whole 4x8x8 slice. The times are simulated.
512 devices in a mesh: seq: 128 (over y, z, core), mp: 4 (over x).
Axes of the slice: x: 4, y: 8, z: 8, core: 2. Of those that a mesh axis runs over, the one named last changes fastest.
Arguments:
- fresh_queries: bfloat16 [8192, 2048], P('seq', 'mp'), may hold values from -120 to 120
- fresh_keys: bfloat16 [8192, 1024], P('seq', 'mp'), may hold values from -6 to 6
- fresh_values: bfloat16 [8192, 1024], P('seq', 'mp'), may hold values from -6 to 6
- cache: bfloat16 [2, 8192, 1024], P(None, 'seq', 'mp'), may hold values from -6 to 6
- pool_root: int32 [128, 32], replicated, may hold values from 0 to 31
- branch_owner: int32 [128], replicated, may hold values from 0 to 127, each once
- branch_len: int32 [128], replicated, may hold values from 1 to 32, 2048 in all
- branch_root: int32 [128], replicated, may hold values from 0 to 31
- request_branch: int32 [128, 4], P('seq'), may hold values from 0 to 127
- token_request: int32 [128, 64], P('seq'), may hold values from 0 to 3, never falling along the last dimension, each value on 1 to 32 neighbouring positions
- residual: bfloat16 [8192, 2048], P('seq'), may hold values from -1.5 to 1.5
- wo_t: bfloat16 [2048, 2048], P('seq', 'mp'), may hold values from -0.125 to 0.125
- norm_gain: float32 [2048], replicated, may hold values from 0.1 to 1.9
- w_qkv: bfloat16 [2048, 4096], P('seq', 'mp'), may hold values from -0.125 to 0.125
Outputs:
- attn: bfloat16 [8192, 2048], P('seq', 'mp')
- stream: bfloat16 [8192, 2048], P('seq')
- qkv_next: bfloat16 [8192, 4096], P('seq', 'mp')
Inputs may be any that keep to these rules, and one draw needn't show every extreme that they name: `token_request`: in each index's row the request number never falls, and each request has 1 to 32 tokens. `branch_owner`: each index of seq holds exactly one branch. `branch_len`: the longest branch has 32 rows.
All inputs are finite; a program needn't handle non-finite values.
Results may differ from a plain program's by a relative error of at most 0.018.
Values may be sent and summed in bfloat16 or wider, within the bound.
A program may use at most 64 MiB of HBM per device.

v0:
```python
import jax
import jax.numpy as jnp
from jax import lax
from jax.sharding import PartitionSpec as P

QUERY_HEADS = 16
KEY_VALUE_HEADS = 8
HEAD_SIZE = 128


def cache_tags(pool_root, branch_owner, branch_len, root_count, slot_count):
    owner_count = pool_root.shape[0]
    branch_count = branch_owner.shape[0]
    branch_ids = jnp.arange(branch_count, dtype=jnp.int32)
    owner_ids = jnp.arange(owner_count, dtype=jnp.int32)
    owned = jnp.sum(
        jnp.where(branch_owner[None, :] == owner_ids[:, None], branch_ids[None, :], 0), axis=1
    )
    owned_length = jnp.sum(
        jnp.where(branch_ids[None, :] == owned[:, None], branch_len[None, :], 0), axis=1
    )
    slot_ids = jnp.arange(slot_count, dtype=jnp.int32)
    branch_tags = jnp.where(
        slot_ids[None, :] < owned_length[:, None], root_count + owned[:, None], -1
    )
    return jnp.concatenate([pool_root, branch_tags], axis=1).reshape(-1)


def absorb(running, query_rows, key_row_block, value_rows, visible, score_scale):
    peak_old, total, mixed = running
    scores = (
        jnp.einsum("tkgd,rkd->tkgr", query_rows, key_row_block, preferred_element_type=jnp.float32)
        * score_scale
    )
    seen = visible[:, None, None, :]
    peak_new = jnp.maximum(peak_old, jnp.max(jnp.where(seen, scores, -jnp.inf), axis=-1))
    factor = jnp.exp(peak_old - peak_new)
    weights_full = jnp.where(seen, jnp.exp(scores - peak_new[..., None]), 0.0)
    total = total * factor + jnp.sum(weights_full, axis=-1)
    mixed = mixed * factor[..., None] + jnp.einsum(
        "tkgr,rkd->tkgd",
        weights_full.astype(jnp.bfloat16),
        value_rows,
        preferred_element_type=jnp.float32,
    )
    return (peak_new, total, mixed)


def on_device(
    fresh_queries,
    fresh_keys,
    fresh_values,
    cache,
    pool_root,
    branch_owner,
    branch_len,
    branch_root,
    request_branch,
    token_request,
    residual,
    wo_t,
    norm_gain,
    w_qkv,
):
    seq_count = lax.axis_size("seq")
    root_count = seq_count // 4
    tok_rows = fresh_queries.shape[0]
    kv_local = fresh_keys.shape[1] // HEAD_SIZE
    query_groups = QUERY_HEADS // KEY_VALUE_HEADS
    score_scale = HEAD_SIZE ** (-0.5)
    slot_count = cache.shape[1] - pool_root.shape[1]
    tags = cache_tags(pool_root, branch_owner, branch_len, root_count, slot_count)
    requests = token_request[0]
    local_branches = request_branch[0]
    request_ids = jnp.arange(local_branches.shape[0], dtype=jnp.int32)
    token_branch = jnp.sum(
        jnp.where(requests[:, None] == request_ids[None, :], local_branches[None, :], 0), axis=1
    )
    branch_ids = jnp.arange(branch_root.shape[0], dtype=jnp.int32)
    token_root = jnp.sum(
        jnp.where(token_branch[:, None] == branch_ids[None, :], branch_root[None, :], 0), axis=1
    )
    query_rows = fresh_queries.reshape(tok_rows, kv_local, query_groups, HEAD_SIZE)
    incoming_keys = fresh_keys.reshape(tok_rows, kv_local, HEAD_SIZE)
    incoming_values = fresh_values.reshape(tok_rows, kv_local, HEAD_SIZE)
    positions = jnp.arange(tok_rows, dtype=jnp.int32)
    own_visible = (requests[None, :] == requests[:, None]) & (
        positions[None, :] <= positions[:, None]
    )
    start_state = (
        jnp.full((tok_rows, kv_local, query_groups), -jnp.inf, jnp.float32),
        jnp.zeros((tok_rows, kv_local, query_groups), jnp.float32),
        jnp.zeros((tok_rows, kv_local, query_groups, HEAD_SIZE), jnp.float32),
    )
    start_state = absorb(
        start_state, query_rows, incoming_keys, incoming_values, own_visible, score_scale
    )
    state = start_state
    piece = lax.all_gather(cache, "seq", axis=1, tiled=True)
    rows = piece.shape[1]
    block = 512
    key_blocks = piece[0].reshape(rows // block, block, kv_local, HEAD_SIZE)
    value_blocks = piece[1].reshape(rows // block, block, kv_local, HEAD_SIZE)
    tag_blocks = tags.reshape(rows // block, block)

    def one_block(running, parts):
        key_row_block, value_rows, tag_rows = parts
        visible = (tag_rows[None, :] == token_root[:, None]) | (
            tag_rows[None, :] == root_count + token_branch[:, None]
        )
        updated = absorb(running, query_rows, key_row_block, value_rows, visible, score_scale)
        return (updated, None)

    state, unused = lax.scan(one_block, state, (key_blocks, value_blocks, tag_blocks))
    peak_final, total_final, mixed_final = state
    attn = (
        (mixed_final / total_final[..., None])
        .reshape(tok_rows, kv_local * query_groups * HEAD_SIZE)
        .astype(jnp.bfloat16)
    )
    partial_value = lax.dot_general(
        attn,
        lax.all_gather(wo_t, "seq", axis=0, tiled=True),
        (((1,), (1,)), ((), ())),
        preferred_element_type=jnp.float32,
    )
    summed = lax.psum(partial_value.astype(jnp.bfloat16), "mp").astype(jnp.float32)
    stream = (residual.astype(jnp.float32) + summed).astype(jnp.bfloat16)
    widened = stream.astype(jnp.float32)
    mean_square = jnp.mean(widened * widened, axis=-1, keepdims=True)
    normed = (widened * lax.rsqrt(mean_square + 1e-06) * norm_gain[None, :]).astype(jnp.bfloat16)
    qkv_sum = jnp.dot(
        normed, lax.all_gather(w_qkv, "seq", axis=0, tiled=True), preferred_element_type=jnp.float32
    )
    return (attn, stream, qkv_sum.astype(jnp.bfloat16))


def solution(mesh):
    return jax.shard_map(
        on_device,
        mesh=mesh,
        in_specs=(
            P("seq", "mp"),
            P("seq", "mp"),
            P("seq", "mp"),
            P(None, "seq", "mp"),
            P(),
            P(),
            P(),
            P(),
            P("seq", None),
            P("seq", None),
            P("seq", None),
            P("seq", "mp"),
            P(),
            P("seq", "mp"),
        ),
        out_specs=(P("seq", "mp"), P("seq", None), P("seq", "mp")),
        check_vma=False,
    )
```

profile of v0, /device:TPU:1, one launch (start us, length us, event | category | flops | bytes accessed | tf_op | source)
XLA Modules:
  0.0 339.6 jit_solution(17679690994480268077)
XLA Ops:
  16.6 88.7 %all-gather.4.cloned.1.call-done = bf16[2,8192,256]{2,1,0:T(8,128)(2,1)} async-done(((bf16[2,64,256]{2,1,0:T(8,128)(2,1)}), bf16[2,8192,256]{2,1,0:T(8,128)(2,1)}) %all-gather.4.cloned.1.call-update) | async-done | bytes 8388624 | tf_op jit(solution)/shard_map/all_gather | solution.py:99
  105.3 5.7 %fusion.30 = (bf16[1,8192,256]{2,1,0:T(8,128)(2,1)}, bf16[1,8192,256]{2,1,0:T(8,128)(2,1)}) fusion(bf16[2,8192,256]{2,1,0:T(8,128)(2,1)} %all-gather.4.cloned.1.call-done), kind=kLoop, calls=%fused_computation.64 | loop fusion | bytes 16777216 | tf_op jit(solution)/shard_map/slice | solution.py:103
  111.0 6.9 %reshape.143 = bf16[16,512,2,128]{3,2,1,0:T(2,128)(2,1)} reshape(bf16[1,8192,256]{2,1,0:T(8,128)(2,1)} %get-tuple-element.107) | data formatting | bytes 8388608 | tf_op jit(solution)/shard_map/reshape;squeeze | solution.py:102
  118.0 6.9 %reshape.144 = bf16[16,512,2,128]{3,2,1,0:T(2,128)(2,1)} reshape(bf16[1,8192,256]{2,1,0:T(8,128)(2,1)} %get-tuple-element.106) | data formatting | bytes 8388608 | tf_op jit(solution)/shard_map/reshape;squeeze | solution.py:103
  124.9 39.2 %while.14 = (s32[]{:T(128)}, f32[64,2,2]{0,2,1:T(2,128)S(1)}, f32[64,2,2]{0,2,1:T(2,128)S(1)}, f32[64,2,2,128]{3,0,2,1:T(8,128)S(1)}, s32[16,512]{1,0:T(8,128)S(...) while((s32[]{:T(128)}, f32[64,2,2]{0,2,1:T(2,128)S(1)}, ...), condition=%wide.region_9.10_spmd, body=%wide.region_6.9_spmd.sunk | while | flops 68452928 | bytes 3628149 | solution.py:114
  125.0 1.4 constant_dynamic-slice_fusion.6
  127.5 1.4 constant_dynamic-slice_fusion.6
  129.9 1.4 constant_dynamic-slice_fusion.6
  132.4 1.4 constant_dynamic-slice_fusion.6
  134.8 1.4 constant_dynamic-slice_fusion.6
  137.3 1.4 constant_dynamic-slice_fusion.6
  139.7 1.4 constant_dynamic-slice_fusion.6
  142.2 1.4 constant_dynamic-slice_fusion.6
  144.6 1.4 constant_dynamic-slice_fusion.6
  147.1 1.4 constant_dynamic-slice_fusion.6
  149.5 1.4 constant_dynamic-slice_fusion.6
  152.0 1.4 constant_dynamic-slice_fusion.6
  154.4 1.4 constant_dynamic-slice_fusion.6
  159.3 1.4 constant_dynamic-slice_fusion.6
  164.3 23.8 %all-gather.6.cloned.1.call-done = bf16[2048,512]{1,0:T(8,128)(2,1)} async-done(((bf16[16,512]{1,0:T(8,128)(2,1)}), bf16[2048,512]{1,0:T(8,128)(2,1)}) %all-gather.6.cloned.1.call-update) | async-done | bytes 2097168 | tf_op jit(solution)/shard_map/all_gather | solution.py:123
  188.1 3.0 convolution_convert_fusion
  191.8 46.3 %all-reduce.2.cloned.1.call-done = bf16[64,2048]{1,0:T(8,128)(2,1)} async-done(((bf16[64,2048]{1,0:T(8,128)(2,1)}), bf16[64,2048]{1,0:T(8,128)(2,1)}) %all-reduce.2.cloned.1.call-update) | async-done | bytes 262160 | tf_op jit(solution)/shard_map/psum | solution.py:127
  239.3 90.1 %all-gather.8.cloned.1.call-done = bf16[2048,1024]{1,0:T(8,128)(2,1)} async-done(((bf16[16,1024]{1,0:T(8,128)(2,1)}), bf16[2048,1024]{1,0:T(8,128)(2,1)}) %all-gather.8.cloned.1.call-update) | async-done | bytes 4194320 | tf_op jit(solution)/shard_map/all_gather | solution.py:133
  329.3 3.7 %convolution_convert_fusion.1 = bf16[64,1024]{1,0:T(8,128)(2,1)} fusion(bf16[2048,1024]{1,0:T(8,128)(2,1)} %all-gather.8.cloned.1.call-done, bf16[64,2048]{1,0:T(8,128)(2,1)S(1)} %get-tuple-element.101, f32[2048]{0:T(1024)S(1)} %copy-done.3, f32[64]{0:T(128)S(1)} %add_rsqrt_fusion), kind=kOutput, calls=%fused_computation.22 | convolution fusion | flops 269025280 | bytes 4595968 | tf_op jit(solution)/shard_map/dot_general | solution.py:132
  (185 shorter events, 29.8 us)
Async XLA Ops:
  7.2 98.1 %all-gather.4.cloned.1.call-start = ((), (), s32[]{:S(2)}) async-start(), calls=%async_computation | async-start | bytes 8454144 | tf_op jit(solution)/shard_map/all_gather | solution.py:99
  7.9 180.2 %all-gather.6.cloned.1.call-start = ((), (), s32[]{:S(2)}) async-start(), calls=%async_computation.1 | async-start | bytes 2113536 | tf_op jit(solution)/shard_map/all_gather | solution.py:123
  8.6 229.4 %all-reduce.2.cloned.1.call-start = ((), (), s32[]{:S(2)}) async-start(), calls=%async_computation.2 | async-start | bytes 524288 | tf_op jit(solution)/shard_map/psum | solution.py:127
  124.9 113.2 %copy-start.2 = (bf16[64,2048]{1,0:T(8,128)(2,1)S(1)}, bf16[64,2048]{1,0:T(8,128)(2,1)}, u32[]{:S(2)}) copy-start(bf16[64,2048]{1,0:T(8,128)(2,1)} %param.26) | copy-start | bytes 786436
  124.9 204.4 %copy-start.3 = (f32[2048]{0:T(1024)S(1)}, f32[2048]{0:T(1024)}, u32[]{:S(2)}) copy-start(f32[2048]{0:T(1024)} %param.28) | copy-start | bytes 24580
  164.3 168.7 %copy-start.1 = (bf16[64,512]{1,0:T(8,128)(2,1)}, bf16[64,512]{1,0:T(8,128)(2,1)S(1)}, u32[]{:S(2)}) copy-start(bf16[64,512]{1,0:T(8,128)(2,1)S(1)} %convert_element_type.35) | copy-start | bytes 196612
  191.2 138.1 %all-gather.8.cloned.1.call-start = ((), (), s32[]{:S(2)}) async-start(), calls=%async_computation.3 | async-start | bytes 4227072 | tf_op jit(solution)/shard_map/all_gather | solution.py:133
  239.2 93.8 %copy-start = (bf16[64,2048]{1,0:T(8,128)(2,1)}, bf16[64,2048]{1,0:T(8,128)(2,1)S(1)}, u32[]{:S(2)}) copy-start(bf16[64,2048]{1,0:T(8,128)(2,1)S(1)} %get-tuple-element.101) | copy-start | bytes 786436
Sparse Core Ops, SparseCore 0:
  11.2 94.0 all-gather.3
  108.4 79.6 all-gather.5
  191.3 46.7 all-reduce.1
  241.5 87.7 all-gather.7
where the time goes:
time: 341 us; the launch traced here: 340 us
  waiting for transfers between devices  251 us (74%)
  local copies, waits for them, and re-layouts  44.9 us (13%)
  matrix products  17.1 us (5%)
  between operations  13.9 us (4%)
  other arithmetic  11.8 us (3%)
    all_gather x1, waiting for transfers between devices, on_device(): lax.all_gather(w_qkv, 'seq', axis=0, tiled=True)  90.1 us
    all_gather x1, waiting for transfers between devices, on_device(): piece = lax.all_gather(cache, 'seq', axis=1, tiled=True)  88.7 us
    psum x1, waiting for transfers between devices, on_device(): lax.psum(partial_value.astype(jnp.bfloat16), 'mp').astype(jnp.float32)  46.3 us
    all_gather x1, waiting for transfers between devices, on_device(): lax.all_gather(wo_t, 'seq', axis=0, tiled=True)  23.8 us
    dynamic_slice x32, local copies, waits for them, and re-layouts, on_device(): lax.scan(one_block, state, (key_blocks, value_blocks, tag_blocks))  22.5 us
    another operation x1, local copies, waits for them, and re-layouts, on_device(): value_blocks = piece[1].reshape(rows // block, block, kv_local, HEAD_SIZE)  6.94 us
    another operation x1, local copies, waits for them, and re-layouts, on_device(): key_blocks = piece[0].reshape(rows // block, block, kv_local, HEAD_SIZE)  6.93 us
  transfers between devices with their start and end apart: 4, of which 4 were waited for; matrix products, arithmetic and copies ran while one was open for 20% of the time, Pallas kernels for 0%

commit v1 on v0

--- a/solution.py
+++ b/solution.py
@@ -124,7 +124,9 @@
         (((1,), (1,)), ((), ())),
         preferred_element_type=jnp.float32,
     )
-    summed = lax.psum(partial_value.astype(jnp.bfloat16), "mp").astype(jnp.float32)
+    summed = jnp.sum(lax.all_gather(partial_value.astype(jnp.bfloat16), "mp"), axis=0).astype(
+        jnp.float32
+    )
     stream = (residual.astype(jnp.float32) + summed).astype(jnp.bfloat16)
     widened = stream.astype(jnp.float32)
     mean_square = jnp.mean(widened * widened, axis=-1, keepdims=True)

time: 341 us -> 317 us (0.930)
  waiting for transfers between devices: 251 us -> 227 us
    psum x1 -> x0, waiting for transfers between devices: 46.3 us -> none  [on_device(): lax.psum(partial_value.astype(jnp.bfloat16), 'mp').astype(jnp.float32)]
    all_gather x0 -> x1, waiting for transfers between devices: none -> 24.5 us  [on_device(): lax.all_gather(partial_value.astype(jnp.bfloat16), 'mp')]
  transfers between devices with their start and end apart: 4 -> 4, of which waited for: 4 -> 4; matrix products, arithmetic and copies ran while one was open for 20% -> 21% of each run, Pallas kernels for 0% -> 0%
where the time goes in v1:
time: 317 us; the launch traced here: 316 us
  waiting for transfers between devices  227 us (72%)
  local copies, waits for them, and re-layouts  44.9 us (14%)
  matrix products  17.1 us (5%)
  between operations  13.9 us (4%)
  other arithmetic  12.2 us (4%)
    all_gather x1, waiting for transfers between devices, on_device(): piece = lax.all_gather(cache, 'seq', axis=1, tiled=True)  88.7 us
    all_gather x1, waiting for transfers between devices, on_device(): lax.all_gather(w_qkv, 'seq', axis=0, tiled=True)  87.8 us
    all_gather x1, waiting for transfers between devices, on_device(): lax.all_gather(partial_value.astype(jnp.bfloat16), 'mp')  24.5 us
    all_gather x1, waiting for transfers between devices, on_device(): lax.all_gather(wo_t, 'seq', axis=0, tiled=True)  23.8 us
    dynamic_slice x32, local copies, waits for them, and re-layouts, on_device(): lax.scan(one_block, state, (key_blocks, value_blocks, tag_blocks))  22.5 us
    another operation x1, local copies, waits for them, and re-layouts, on_device(): value_blocks = piece[1].reshape(rows // block, block, kv_local, HEAD_SIZE)  6.94 us
    another operation x1, local copies, waits for them, and re-layouts, on_device(): key_blocks = piece[0].reshape(rows // block, block, kv_local, HEAD_SIZE)  6.93 us
  transfers between devices with their start and end apart: 4, of which 4 were waited for; matrix products, arithmetic and copies ran while one was open for 21% of the time, Pallas kernels for 0%

profile of v1, /device:TPU:1, one launch (start us, length us, event | category | flops | bytes accessed | tf_op | source)
XLA Modules:
  0.0 315.9 jit_solution(10277070558923110238)
XLA Ops:
  16.6 88.7 %all-gather.6.cloned.1.call-done = bf16[2,8192,256]{2,1,0:T(8,128)(2,1)} async-done(((bf16[2,64,256]{2,1,0:T(8,128)(2,1)}), bf16[2,8192,256]{2,1,0:T(8,128)(2,1)}) %all-gather.6.cloned.1.call-update) | async-done | bytes 8388624 | tf_op jit(solution)/shard_map/all_gather | solution.py:99
  105.3 5.7 %fusion.30 = (bf16[1,8192,256]{2,1,0:T(8,128)(2,1)}, bf16[1,8192,256]{2,1,0:T(8,128)(2,1)}) fusion(bf16[2,8192,256]{2,1,0:T(8,128)(2,1)} %all-gather.6.cloned.1.call-done), kind=kLoop, calls=%fused_computation.64 | loop fusion | bytes 16777216 | tf_op jit(solution)/shard_map/slice | solution.py:103
  111.0 6.9 %reshape.144 = bf16[16,512,2,128]{3,2,1,0:T(2,128)(2,1)} reshape(bf16[1,8192,256]{2,1,0:T(8,128)(2,1)} %get-tuple-element.107) | data formatting | bytes 8388608 | tf_op jit(solution)/shard_map/reshape;squeeze | solution.py:102
  118.0 6.9 %reshape.145 = bf16[16,512,2,128]{3,2,1,0:T(2,128)(2,1)} reshape(bf16[1,8192,256]{2,1,0:T(8,128)(2,1)} %get-tuple-element.106) | data formatting | bytes 8388608 | tf_op jit(solution)/shard_map/reshape;squeeze | solution.py:103
  124.9 39.2 %while.14 = (s32[]{:T(128)}, f32[64,2,2]{0,2,1:T(2,128)S(1)}, f32[64,2,2]{0,2,1:T(2,128)S(1)}, f32[64,2,2,128]{3,0,2,1:T(8,128)S(1)}, s32[16,512]{1,0:T(8,128)S(...) while((s32[]{:T(128)}, f32[64,2,2]{0,2,1:T(2,128)S(1)}, ...), condition=%wide.region_9.10_spmd, body=%wide.region_6.9_spmd.sunk | while | flops 68452928 | bytes 3628149 | solution.py:114
  125.0 1.4 constant_dynamic-slice_fusion.6
  127.5 1.4 constant_dynamic-slice_fusion.6
  129.9 1.4 constant_dynamic-slice_fusion.6
  132.4 1.4 constant_dynamic-slice_fusion.6
  134.8 1.4 constant_dynamic-slice_fusion.6
  137.3 1.4 constant_dynamic-slice_fusion.6
  139.7 1.4 constant_dynamic-slice_fusion.6
  142.2 1.4 constant_dynamic-slice_fusion.6
  144.6 1.4 constant_dynamic-slice_fusion.6
  147.1 1.4 constant_dynamic-slice_fusion.6
  149.5 1.4 constant_dynamic-slice_fusion.6
  152.0 1.4 constant_dynamic-slice_fusion.6
  159.3 1.4 constant_dynamic-slice_fusion.6
  164.4 23.8 %all-gather.8.cloned.1.call-done = bf16[2048,512]{1,0:T(8,128)(2,1)} async-done(((bf16[16,512]{1,0:T(8,128)(2,1)}), bf16[2048,512]{1,0:T(8,128)(2,1)}) %all-gather.8.cloned.1.call-update) | async-done | bytes 2097168 | tf_op jit(solution)/shard_map/all_gather | solution.py:123
  188.1 3.0 convolution_convert_fusion
  191.8 24.5 %all-gather.12.cloned.1.call-done = bf16[256,2048]{1,0:T(8,128)(2,1)} async-done(((bf16[64,2048]{1,0:T(8,128)(2,1)}), bf16[256,2048]{1,0:T(8,128)(2,1)}) %all-gather.12.cloned.1.call-update) | async-done | bytes 1048592 | tf_op jit(solution)/shard_map/all_gather | solution.py:127
  216.2 1.4 reduce_sum.80
  217.9 87.8 %all-gather.10.cloned.1.call-done = bf16[2048,1024]{1,0:T(8,128)(2,1)} async-done(((bf16[16,1024]{1,0:T(8,128)(2,1)}), bf16[2048,1024]{1,0:T(8,128)(2,1)}) %all-gather.10.cloned.1.call-update) | async-done | bytes 4194320 | tf_op jit(solution)/shard_map/all_gather | solution.py:135
  305.6 3.7 %convolution_convert_fusion.1 = bf16[64,1024]{1,0:T(8,128)(2,1)} fusion(bf16[2048,1024]{1,0:T(8,128)(2,1)} %all-gather.10.cloned.1.call-done, bf16[64,2048]{1,0:T(8,128)(2,1)S(1)} %get-tuple-element.101, f32[2048]{0:T(1024)S(1)} %copy-done.3, f32[64]{0:T(128)S(1)} %add_rsqrt_fusion), kind=kOutput, calls=%fused_computation.22 | convolution fusion | flops 269025280 | bytes 4595968 | tf_op jit(solution)/shard_map/dot_general | solution.py:134
  (186 shorter events, 30.3 us)
Async XLA Ops:
  7.2 98.1 %all-gather.6.cloned.1.call-start = ((), (), s32[]{:S(2)}) async-start(), calls=%async_computation | async-start | bytes 8454144 | tf_op jit(solution)/shard_map/all_gather | solution.py:99
  7.9 180.2 %all-gather.8.cloned.1.call-start = ((), (), s32[]{:S(2)}) async-start(), calls=%async_computation.1 | async-start | bytes 2113536 | tf_op jit(solution)/shard_map/all_gather | solution.py:123
  8.6 207.6 %all-gather.12.cloned.1.call-start = ((), (), s32[]{:S(2)}) async-start(), calls=%async_computation.3 | async-start | bytes 1310720 | tf_op jit(solution)/shard_map/all_gather | solution.py:127
  164.1 53.6 %copy-start.2 = (bf16[64,2048]{1,0:T(8,128)(2,1)S(1)}, bf16[64,2048]{1,0:T(8,128)(2,1)}, u32[]{:S(2)}) copy-start(bf16[64,2048]{1,0:T(8,128)(2,1)} %param.26) | copy-start | bytes 786436
  164.1 141.5 %copy-start.3 = (f32[2048]{0:T(1024)S(1)}, f32[2048]{0:T(1024)}, u32[]{:S(2)}) copy-start(f32[2048]{0:T(1024)} %param.28) | copy-start | bytes 24580
  164.3 145.0 %copy-start.1 = (bf16[64,512]{1,0:T(8,128)(2,1)}, bf16[64,512]{1,0:T(8,128)(2,1)S(1)}, u32[]{:S(2)}) copy-start(bf16[64,512]{1,0:T(8,128)(2,1)S(1)} %convert_element_type.37) | copy-start | bytes 196612
  191.2 114.4 %all-gather.10.cloned.1.call-start = ((), (), s32[]{:S(2)}) async-start(), calls=%async_computation.2 | async-start | bytes 4227072 | tf_op jit(solution)/shard_map/all_gather | solution.py:135
  217.9 91.5 %copy-start = (bf16[64,2048]{1,0:T(8,128)(2,1)}, bf16[64,2048]{1,0:T(8,128)(2,1)S(1)}, u32[]{:S(2)}) copy-start(bf16[64,2048]{1,0:T(8,128)(2,1)S(1)} %get-tuple-element.101) | copy-start | bytes 786436
Sparse Core Ops, SparseCore 0:
  11.2 94.0 all-gather.5
  108.4 79.6 all-gather.7
  191.3 24.8 all-gather.11
  219.2 86.3 all-gather.9
